TPU v7x, 256 devices: a whole 4x4x8 slice. The times are simulated.
256 devices in a mesh: ctx: 32 (over z, x), tp: 8 (over y, core).
Axes of the slice: x: 4, y: 4, z: 8, core: 2. Of those that a mesh axis runs over, the one named last changes fastest.
Arguments:
- attn_query: bfloat16 [8192, 4096], P('ctx', 'tp'), may hold values from -8 to 8
- attn_key: bfloat16 [8192, 4096], P('ctx', 'tp'), may hold values from -8 to 8
- attn_value: bfloat16 [8192, 4096], P('ctx', 'tp'), may hold values from -6 to 6
- out_weight: bfloat16 [4096, 8192], P('tp'), may hold values from -0.125 to 0.125
Outputs:
- attn_out: bfloat16 [8192, 8192], P('ctx', 'tp')
All inputs are finite; a program needn't handle non-finite values.
Results may differ from a plain program's by a relative error of at most 0.015.
Values may be sent and summed in bfloat16 or wider, within the bound.
A program may use at most 128 MiB of HBM per device.

v0:
```python
import jax
import jax.numpy as jnp
from jax import lax
from jax.sharding import PartitionSpec as P

HD = 128


def attend(queries, keys, values, query_pos, key_position):
    rows = queries.shape[0]
    local_heads = queries.shape[1] // HD
    scale = HD ** (-0.5)
    shaped_q = queries.reshape(rows, local_heads, HD)
    latest = jnp.max(query_pos)
    initial = (
        jnp.full((local_heads, rows), -1e30, jnp.float32),
        jnp.zeros((local_heads, rows), jnp.float32),
        jnp.zeros((local_heads, rows, HD), jnp.float32),
    )
    piece_keys = lax.all_gather(keys, "ctx", axis=0, tiled=True)
    piece_values = lax.all_gather(values, "ctx", axis=0, tiled=True)
    count_rows = piece_keys.shape[0]
    span_rows = 512

    def one_block(block, state):
        offset = block * span_rows
        block_keys = lax.dynamic_slice_in_dim(piece_keys, offset, span_rows, 0).reshape(
            span_rows, local_heads, HD
        )
        block_values = lax.dynamic_slice_in_dim(piece_values, offset, span_rows, 0).reshape(
            span_rows, local_heads, HD
        )
        key_pos = key_position(offset + jnp.arange(span_rows, dtype=jnp.int32))

        def compute(inner):
            maxes, totals, accum = inner
            scores = (
                jnp.einsum("qhd,khd->hqk", shaped_q, block_keys, preferred_element_type=jnp.float32)
                * scale
            )
            allowed = key_pos[None, None, :] <= query_pos[None, :, None]
            new_max = jnp.maximum(maxes, jnp.max(jnp.where(allowed, scores, -1e30), axis=-1))
            factor = jnp.exp(maxes - new_max)
            weights = jnp.where(allowed, jnp.exp(scores - new_max[..., None]), 0.0)
            totals = totals * factor + jnp.sum(weights, axis=-1)
            accum = accum * factor[..., None] + jnp.einsum(
                "hqk,khd->hqd",
                weights.astype(jnp.bfloat16),
                block_values,
                preferred_element_type=jnp.float32,
            )
            return (new_max, totals, accum)

        def keep(inner):
            return inner

        return lax.cond(jnp.min(key_pos) <= latest, compute, keep, state)

    maxes, totals, accum = lax.fori_loop(0, count_rows // span_rows, one_block, initial)
    result = accum / totals[..., None]
    return jnp.transpose(result, (1, 0, 2)).reshape(rows, local_heads * HD).astype(jnp.bfloat16)


def per_device(attn_query, attn_key, attn_value, out_weight):
    index = lax.axis_index("ctx")
    rows = attn_query.shape[0]
    local_rows = jnp.arange(rows, dtype=jnp.int32)
    query_pos = index * rows + local_rows

    def key_position(global_rows):
        return global_rows

    heads = attend(attn_query, attn_key, attn_value, query_pos, key_position)
    partial_value = jnp.dot(heads, out_weight, preferred_element_type=jnp.float32).astype(
        jnp.bfloat16
    )
    partial_value = lax.optimization_barrier(partial_value).astype(jnp.float32)
    attn_out = lax.psum_scatter(
        partial_value.astype(jnp.bfloat16), "tp", scatter_dimension=1, tiled=True
    )
    return attn_out


def solution(mesh):
    return jax.shard_map(
        per_device,
        mesh=mesh,
        in_specs=(P("ctx", "tp"), P("ctx", "tp"), P("ctx", "tp"), P("tp", None)),
        out_specs=P("ctx", "tp"),
        check_vma=False,
    )
```

profile of v0, /device:TPU:1, one launch (start us, length us, event | category | flops | bytes accessed | tf_op | source)
XLA Modules:
  0.0 355.3 jit_solution(11459322073344142620)
XLA Ops:
  6.5 0.0 all-gather.3.cloned.1.call-start
  6.5 1.8 copy.9
  8.3 0.0 all-gather.3.cloned.1.call-update
  8.4 0.0 all-gather.5.cloned.1.call-start
  8.4 1.8 copy.11
  10.2 0.0 all-gather.5.cloned.1.call-update
  10.2 0.0 reduce-scatter.2.cloned.1.call-start
  10.3 0.6 add_reduce_fusion
  10.9 1.1 copy.10
  12.0 0.2 copy.12
  12.2 102.7 %all-gather.3.cloned.1.call-done = bf16[8192,512]{0,1:T(8,128)(2,1)} async-done(((bf16[256,512]{0,1:T(8,128)(2,1)}), bf16[8192,512]{0,1:T(8,128)(2,1)}) %all-gather.3.cloned.1.call-update) | async-done | bytes 8388624 | tf_op jit(solution)/shard_map/all_gather | solution.py:20
  114.8 103.7 %all-gather.5.cloned.1.call-done = bf16[8192,512]{0,1:T(8,128)(2,1)} async-done(((bf16[256,512]{0,1:T(8,128)(2,1)}), bf16[8192,512]{0,1:T(8,128)(2,1)}) %all-gather.5.cloned.1.call-update) | async-done | bytes 8388624 | tf_op jit(solution)/shard_map/all_gather | solution.py:21
  218.6 34.0 %while.18 = (s32[]{:T(128)}, f32[4,256]{1,0:T(4,128)S(1)}, f32[4,256]{1,0:T(4,128)S(1)}, f32[4,256,128]{2,1,0:T(8,128)S(1)}, s32[]{:T(128)}, /*index=5*/bf16[819...) while((s32[]{:T(128)}, f32[4,256]{1,0:T(4,128)S(1)}, ...), condition=%wide.region_7.8_spmd.clone, body=%wide.region_1.7_spmd.clone.sunk | while | flops 274599168 | bytes 11346241 | solution.py:59
  218.6 0.7 iota_add_fusion.2
  220.5 3.4 conditional.3
  220.5 0.1 broadcast_compare_fusion
  220.7 1.3 constant_dynamic-slice_fusion
  222.0 0.6 fusion.2
  222.6 0.5 fusion.6
  223.0 0.9 convolution_add_fusion
  224.0 0.7 iota_add_fusion.2
  225.9 0.7 iota_add_fusion.2
  227.8 0.7 iota_add_fusion.2
  229.7 0.7 iota_add_fusion.2
  231.6 0.7 iota_add_fusion.2
  233.5 0.7 iota_add_fusion.2
  235.4 0.7 iota_add_fusion.2
  237.3 0.7 iota_add_fusion.2
  239.3 0.7 iota_add_fusion.2
  241.2 0.7 iota_add_fusion.2
  243.1 0.7 iota_add_fusion.2
  245.0 0.7 iota_add_fusion.2
  246.9 0.7 iota_add_fusion.2
  248.8 0.7 iota_add_fusion.2
  250.7 0.7 iota_add_fusion.2
  252.6 0.2 copy.13
  252.9 7.7 %convolution_convert_fusion = bf16[256,8192]{1,0:T(8,128)(2,1)} fusion(bf16[256,512]{0,1:T(8,128)(2,1)S(1)} %bitcast.27, bf16[512,8192]{1,0:T(8,128)(2,1)} %param.11), kind=kOutput, calls=%fused_computation.23 | convolution fusion | flops 2149580800 | bytes 12845056 | tf_op jit(solution)/shard_map/dot_general | solution.py:74
  260.6 0.0 reduce-scatter.2.cloned.1.call-update
  260.6 88.1 %reduce-scatter.2.cloned.1.call-done = bf16[256,1024]{1,0:T(8,128)(2,1)} async-done(((bf16[256,8192]{1,0:T(8,128)(2,1)}), bf16[256,1024]{1,0:T(8,128)(2,1)}) %reduce-scatter.2.cloned.1.call-update) | async-done | bytes 524304 | tf_op jit(solution)/shard_map/reduce_scatter | solution.py:78
  (39 shorter events, 0.4 us)
Async XLA Ops:
  6.5 108.3 %all-gather.3.cloned.1.call-start = ((), (), s32[]{:S(2)}) async-start(), calls=%async_computation.1 | async-start | bytes 8650752 | tf_op jit(solution)/shard_map/all_gather | solution.py:20
  8.4 210.2 %all-gather.5.cloned.1.call-start = ((), (), s32[]{:S(2)}) async-start(), calls=%async_computation.2 | async-start | bytes 8650752 | tf_op jit(solution)/shard_map/all_gather | solution.py:21
  10.2 338.5 %reduce-scatter.2.cloned.1.call-start = ((), (), s32[]{:S(2)}) async-start(), calls=%async_computation.3 | async-start | bytes 4718592 | tf_op jit(solution)/shard_map/reduce_scatter | solution.py:78
Sparse Core Ops, SparseCore 0:
  9.8 104.9 all-gather.2
  117.3 101.2 all-gather.4
  260.7 87.9 reduce-scatter.1
where the time goes:
time: 358 us; the launch traced here: 355 us
  waiting for transfers between devices  295 us (82%)
  loops' own time  20 us (6%)
  between operations  13.2 us (4%)
  other arithmetic  11.9 us (3%)
  matrix products  9.15 us (3%)
  local copies, waits for them, and re-layouts  6.38 us (2%)
    all_gather x1, waiting for transfers between devices, attend(): piece_values = lax.all_gather(values, 'ctx', axis=0, tiled=True)  104 us
    all_gather x1, waiting for transfers between devices, attend(): piece_keys = lax.all_gather(keys, 'ctx', axis=0, tiled=True)  103 us
    reduce_scatter x1, waiting for transfers between devices, per_device(): lax.psum_scatter(partial_value.astype(jnp.bfloat16), 'tp', scatter_dimens...  88.1 us
    another operation x1, loops' own time, attend(): lax.fori_loop(0, count_rows // span_rows, one_block, initial)  19.8 us
    add x16, other arithmetic, one_block(): key_pos = key_position(offset + jnp.arange(span_rows, dtype=jnp.int32))  10.6 us
    dot_general x1, matrix products, per_device(): jnp.dot(heads, out_weight, preferred_element_type=jnp.float32)  7.69 us
  transfers between devices with their start and end apart: 3, of which 3 were waited for; matrix products, arithmetic and copies ran while one was open for 1% of the time, Pallas kernels for 0%

commit v1 on v0

v1 whole, which is shorter than its diff:
```python
import functools

import jax
import jax.numpy as jnp
from jax import lax
from jax.experimental import pallas as pl
from jax.experimental.pallas import tpu as pltpu
from jax.sharding import PartitionSpec as P

HD = 128
NX, NY, NZ, NC = 4, 4, 8, 2
ROWS = 256
HALF = ROWS // NC
COLS = 1024
CHUNK = 256
NCH = COLS // CHUNK
KEYS = NX * ROWS
LOG2E = 1.4426950408889634
C2 = (HD ** -0.5) * LOG2E
F32 = jnp.float32
BF16 = jnp.bfloat16


def wait_for(ref, sem):
    pltpu.make_async_copy(ref, ref, sem).wait()


def kernel(
    q_hbm, k_hbm, v_hbm, w_hbm, out_ref,
    src, qb, kv, wb, heads, obuf, acc, mx, sm, pbuf, ropp, rfin,
    s_load, s_w, r_w, ss_w,
    s_q, s_kv, r_q, r_kv,
    s_x, r_x, s_rel, r_rel,
    s_o, r_o, s_oc, r_oc,
    s_p, r_p,
):
    ctx = lax.axis_index("ctx")
    tp = lax.axis_index("tp")
    z, x = ctx // NX, ctx % NX
    y, c = tp // NC, tp % NC
    xr, xl, xo = (x + 1) % NX, (x + 3) % NX, (x + 2) % NX
    yr, yl, yo = (y + 1) % NY, (y + 3) % NY, (y + 2) % NY
    sib = 1 - c

    def dev(x_, y_, z_, c_):
        return {"ctx": z_ * NX + x_, "tp": y_ * NC + c_}

    def remote(src_ref, dst_ref, send, recv, where):
        return pltpu.make_async_remote_copy(
            src_ref=src_ref, dst_ref=dst_ref, send_sem=send, recv_sem=recv,
            device_id=where, device_id_type=pl.DeviceIdType.MESH,
        )

    right, left, across = dev(xr, y, z, c), dev(xl, y, z, c), dev(x, y, z, sib)
    up, down = dev(x, yr, z, c), dev(x, yl, z, c)

    for n, hbm in enumerate((q_hbm, k_hbm, v_hbm)):
        for j in range(4):
            for h in range(NC):
                pltpu.make_async_copy(
                    hbm.at[pl.ds(h * HALF, HALF), pl.ds(j * HD, HD)], src.at[j, h, n], s_load.at[j, h, n]
                ).start()

    barrier = pltpu.get_barrier_semaphore()
    for k in range(1, NZ * NC):
        other = (z * NC + c + k) % (NZ * NC)
        pl.semaphore_signal(barrier, inc=1, device_id=dev(x, y, other // NC, other % NC), device_id_type=pl.DeviceIdType.MESH)
    for other in (right, left, up, down):
        pl.semaphore_signal(barrier, inc=1, device_id=other, device_id_type=pl.DeviceIdType.MESH)

    acc[...] = jnp.zeros(acc.shape, F32)
    sm[...] = jnp.zeros(sm.shape, F32)
    mx[...] = jnp.full(mx.shape, -1e30, F32)
    for j in range(4):
        for h in range(NC):
            for n in range(3):
                wait_for(src.at[j, h, n], s_load.at[j, h, n])
    pl.semaphore_wait(barrier, NZ * NC - 1 + 4)

    def zof(s):
        return (z + ((s + 1) // 2) * (1 - 2 * ((s + 1) % 2)) + NZ) % NZ

    def send_heads(s, carry):
        zd = zof(s)

        @pl.when(zd // 4 == c)
        def _():
            j = zd - 4 * c
            for k in range(NC):
                cd = (c + 1 - k) % NC

                def go():
                    remote(src.at[j, cd, 0], qb.at[z], s_q.at[j, k], r_q.at[z], dev(x, y, zd, cd)).start()
                    remote(src.at[j, cd, pl.ds(1, 2)], kv.at[z, x * NC + cd], s_kv.at[j, k], r_kv.at[z], dev(x, y, zd, cd)).start()

                if k == 0:
                    go()
                else:
                    pl.when(zd != z)(go)

                    @pl.when(zd == z)
                    def _():
                        pltpu.make_async_copy(src.at[j, cd, 0], qb.at[z], r_q.at[z]).start()
                        pltpu.make_async_copy(src.at[j, cd, pl.ds(1, 2)], kv.at[z, x * NC + cd], r_kv.at[z]).start()

        return carry

    lax.fori_loop(0, NZ, send_heads, 0)

    for n in range(NY):
        pltpu.make_async_copy(
            w_hbm.at[:, pl.ds((n * NC + c) * COLS, COLS)], wb.at[n, c], s_w.at[n]
        ).start()

    def unit(zq, zk, diagonal):
        query = qb[zq]
        key = kv[zk, :, 0].reshape(KEYS, HD)
        value = kv[zk, :, 1].reshape(KEYS, HD)
        scores = lax.dot_general(query, key, (((1,), (1,)), ((), ())), preferred_element_type=F32)
        if diagonal:
            row = lax.broadcasted_iota(jnp.int32, scores.shape, 0)
            col = lax.broadcasted_iota(jnp.int32, scores.shape, 1)
            scores = jnp.where(col <= row + (x * NC + c) * HALF, scores, -1e30)
        old = mx[zq]
        new = jnp.maximum(old, jnp.max(scores, axis=1, keepdims=True))
        factor = jnp.exp2((old - new) * C2)
        weights = jnp.exp2((scores - jnp.concatenate([new] * (KEYS // HD), axis=1)) * C2)
        mx[zq] = new
        sm[zq] = sm[zq] * factor + jnp.sum(weights, axis=1, keepdims=True)
        acc[zq] = acc[zq] * factor + jnp.dot(weights.astype(BF16), value, preferred_element_type=F32)

    def step(s, carry):
        @pl.when(s < NZ)
        def _():
            zs = zof(s)
            mine = kv.at[zs, x * NC + c]
            wait_for(qb.at[zs], r_q.at[zs])
            wait_for(mine, r_kv.at[zs])
            remote(mine, mine, s_x.at[zs, 0], r_x.at[zs, 0], right).start()
            remote(mine, mine, s_x.at[zs, 1], r_x.at[zs, 1], left).start()
            remote(mine, mine, s_rel.at[zs, 0], r_rel.at[zs, 0], across).start()

        @pl.when((s >= 1) & (s < NZ + 1))
        def _():
            zs = zof(s - 1)
            a = kv.at[zs, xl * NC + c]
            wait_for(a, r_x.at[zs, 0])
            remote(a.at[0], a.at[0], s_x.at[zs, 2], r_x.at[zs, 2], right).start()
            remote(a, a, s_rel.at[zs, 1], r_rel.at[zs, 1], across).start()
            b = kv.at[zs, xr * NC + c]
            wait_for(b, r_x.at[zs, 1])
            remote(b.at[1], b.at[1], s_x.at[zs, 3], r_x.at[zs, 3], left).start()
            remote(b, b, s_rel.at[zs, 2], r_rel.at[zs, 2], across).start()

        @pl.when((s >= 2) & (s < NZ + 2))
        def _():
            zs = zof(s - 2)
            o = kv.at[zs, xo * NC + c]
            wait_for(o.at[0], r_x.at[zs, 2])
            wait_for(o.at[1], r_x.at[zs, 3])
            remote(o, o, s_rel.at[zs, 3], r_rel.at[zs, 3], across).start()

        @pl.when((s >= 2) & (s < 2 + NY))
        def _():
            n = s - 2
            remote(
                w_hbm.at[:, pl.ds((n * NC + sib) * COLS, COLS)], wb.at[n, c], ss_w.at[n], r_w.at[n], across
            ).start()

        @pl.when(s >= 3)
        def _():
            t = s - 3
            zs = zof(t)
            for n, xx in enumerate((x, xl, xr, xo)):
                wait_for(kv.at[zs, xx * NC + sib], r_rel.at[zs, n])
            unit(zs, zs, True)

            def earlier(u, inner):
                zu = zof(u)
                unit(jnp.maximum(zs, zu), jnp.minimum(zs, zu), False)
                return inner

            lax.fori_loop(0, t, earlier, 0)

        return carry

    lax.fori_loop(0, NZ + 3, step, 0)

    def send_out(s, carry):
        zs = zof(NZ - 1 - s)
        obuf[zs] = (acc[zs] / sm[zs]).astype(BF16)
        spot = heads.at[pl.ds(c * HALF, HALF), pl.ds(z * HD, HD)]

        @pl.when(zs != z)
        def _():
            remote(obuf.at[zs], spot, s_o.at[zs], r_o.at[z], dev(x, y, zs, c)).start()

        @pl.when(zs == z)
        def _():
            pltpu.make_async_copy(obuf.at[zs], spot, r_o.at[z]).start()

        return carry

    lax.fori_loop(0, NZ, send_out, 0)

    def relay_out(s, carry):
        h = zof(s)
        spot = heads.at[pl.ds(c * HALF, HALF), pl.ds(h * HD, HD)]
        wait_for(spot, r_o.at[h])
        remote(spot, spot, s_oc.at[h], r_oc.at[h], across).start()
        return carry

    lax.fori_loop(0, NZ, relay_out, 0)
    for n in range(NY):
        wait_for(wb.at[n, c], s_w.at[n])
        wait_for(wb.at[n, sib], r_w.at[n])

    def await_out(s, carry):
        h = zof(s)
        wait_for(heads.at[pl.ds(sib * HALF, HALF), pl.ds(h * HD, HD)], r_oc.at[h])
        return carry

    lax.fori_loop(0, NZ, await_out, 0)

    def project(n, k):
        cols = slice(k * CHUNK, (k + 1) * CHUNK)
        weight = jnp.concatenate([wb[n, 0, :, cols], wb[n, 1, :, cols]], axis=0)
        return jnp.dot(heads[...], weight, preferred_element_type=F32)

    for k in range(NCH):
        pbuf[0, k] = project(yo, k).astype(BF16)
        remote(pbuf.at[0, k], ropp.at[k], s_p.at[0, k], r_p.at[0, k], up if k < NCH // 2 else down).start()
    half = NCH // 2
    for k in range(half):
        a, b = half + k, k
        pbuf[1, a] = project(yr, a).astype(BF16)
        remote(pbuf.at[1, a], rfin.at[0, a], s_p.at[1, a], r_p.at[1, a], up).start()
        pbuf[2, b] = project(yl, b).astype(BF16)
        remote(pbuf.at[2, b], rfin.at[1, b], s_p.at[2, b], r_p.at[2, b], down).start()
    for k in range(half):
        a, b = k, half + k
        part = project(yr, a)
        wait_for(ropp.at[a], r_p.at[0, a])
        pbuf[1, a] = (part + ropp[a].astype(F32)).astype(BF16)
        remote(pbuf.at[1, a], rfin.at[0, a], s_p.at[1, a], r_p.at[1, a], up).start()
        part = project(yl, b)
        wait_for(ropp.at[b], r_p.at[0, b])
        pbuf[2, b] = (part + ropp[b].astype(F32)).astype(BF16)
        remote(pbuf.at[2, b], rfin.at[1, b], s_p.at[2, b], r_p.at[2, b], down).start()
    order = [2, 0, 3, 1]
    for k in order:
        part = project(y, k)
        wait_for(rfin.at[0, k], r_p.at[1, k])
        wait_for(rfin.at[1, k], r_p.at[2, k])
        out_ref[:, k * CHUNK : (k + 1) * CHUNK] = (
            part + rfin[0, k].astype(F32) + rfin[1, k].astype(F32)
        ).astype(BF16)

    def drain(s, carry):
        zs = zof(s)

        @pl.when(zs // 4 == c)
        def _():
            j = zs - 4 * c
            wait_for(src.at[j, sib, 0], s_q.at[j, 0])
            wait_for(src.at[j, sib, pl.ds(1, 2)], s_kv.at[j, 0])

            @pl.when(zs != z)
            def _():
                wait_for(src.at[j, c, 0], s_q.at[j, 1])
                wait_for(src.at[j, c, pl.ds(1, 2)], s_kv.at[j, 1])

        for n, xx in enumerate((x, x, xl, xr)):
            part = kv.at[zs, xx * NC + c]
            wait_for(part if n < 2 else part.at[n - 2], s_x.at[zs, n])
        for n, xx in enumerate((x, xl, xr, xo)):
            wait_for(kv.at[zs, xx * NC + c], s_rel.at[zs, n])

        @pl.when(zs != z)
        def _():
            wait_for(obuf.at[zs], s_o.at[zs])

        wait_for(heads.at[pl.ds(c * HALF, HALF), pl.ds(zs * HD, HD)], s_oc.at[zs])
        return carry

    lax.fori_loop(0, NZ, drain, 0)
    for n in range(NY):
        wait_for(w_hbm.at[:, pl.ds((n * NC + sib) * COLS, COLS)], ss_w.at[n])
    for k in range(NCH):
        for n in range(3):
            wait_for(pbuf.at[n, k], s_p.at[n, k])


def per_device(attn_query, attn_key, attn_value, out_weight):
    dma = pltpu.SemaphoreType.DMA
    anywhere = pl.BlockSpec(memory_space=pl.ANY)
    return pl.pallas_call(
        kernel,
        out_shape=jax.ShapeDtypeStruct((ROWS, COLS), BF16),
        in_specs=[anywhere] * 4,
        out_specs=pl.BlockSpec(memory_space=pltpu.VMEM),
        scratch_shapes=[
            pltpu.VMEM((4, NC, 3, HALF, HD), BF16),
            pltpu.VMEM((NZ, HALF, HD), BF16),
            pltpu.VMEM((NZ, NX * NC, 2, HALF, HD), BF16),
            pltpu.VMEM((NY, NC, 512, COLS), BF16),
            pltpu.VMEM((ROWS, NZ * HD), BF16),
            pltpu.VMEM((NZ, HALF, HD), BF16),
            pltpu.VMEM((NZ, HALF, HD), F32),
            pltpu.VMEM((NZ, HALF, HD), F32),
            pltpu.VMEM((NZ, HALF, HD), F32),
            pltpu.VMEM((3, NCH, ROWS, CHUNK), BF16),
            pltpu.VMEM((NCH, ROWS, CHUNK), BF16),
            pltpu.VMEM((2, NCH, ROWS, CHUNK), BF16),
            dma((4, NC, 3)), dma((NY,)), dma((NY,)), dma((NY,)),
            dma((4, NC)), dma((4, NC)), dma((NZ,)), dma((NZ,)),
            dma((NZ, 4)), dma((NZ, 4)), dma((NZ, 4)), dma((NZ, 4)),
            dma((NZ,)), dma((NZ,)), dma((NZ,)), dma((NZ,)),
            dma((3, NCH)), dma((3, NCH)),
        ],
        compiler_params=pltpu.CompilerParams(
            collective_id=0, has_side_effects=True, vmem_limit_bytes=56 << 20
        ),
        name="attention",
    )(attn_query, attn_key, attn_value, out_weight)


def solution(mesh):
    return jax.shard_map(
        per_device,
        mesh=mesh,
        in_specs=(P("ctx", "tp"), P("ctx", "tp"), P("ctx", "tp"), P("tp", None)),
        out_specs=P("ctx", "tp"),
        check_vma=False,
    )
```

time: 358 us -> 87.2 us (0.24)
  waiting for transfers between devices: 295 us -> 0 us
  Pallas kernels: 0 us -> 85.1 us
  loops' own time: 20 us -> 0 us
  between operations: 13.2 us -> 0.01 us
  other arithmetic: 11.9 us -> 0 us
  matrix products: 9.15 us -> 0 us
  local copies, waits for them, and re-layouts: 6.38 us -> 1.87 us
    all_gather x2 -> x0, waiting for transfers between devices: 206 us -> none  [the longest x1 104 us: attend(): piece_values = lax.all_gather(values, 'ctx', axis=0, tiled=True)]
    reduce_scatter x1 -> x0, waiting for transfers between devices: 88.1 us -> none  [per_device(): lax.psum_scatter(partial_value.astype(jnp.bfloat16), 'tp', scatter_dimens...]
    pallas_call x0 -> x1, Pallas kernels: none -> 85.1 us  [per_device(): pl.pallas_call(kernel, out_shape=jax.ShapeDtypeStruct((ROWS, COLS), BF16)...]
    another operation x17 -> x0, loops' own time: 20 us -> none  [the longest x1 19.8 us: attend(): lax.fori_loop(0, count_rows // span_rows, one_block, initial)]
    add x18 -> x0, other arithmetic: 10.6 us -> none  [the longest x16 10.6 us: one_block(): key_pos = key_position(offset + jnp.arange(span_rows, dtype=jnp.int32))]
    dot_general x3 -> x0, matrix products: 9.15 us -> none  [the longest x1 7.69 us: per_device(): jnp.dot(heads, out_weight, preferred_element_type=jnp.float32)]
  transfers between devices with their start and end apart: 3 -> 0, of which waited for: 3 -> 0; matrix products, arithmetic and copies ran while one was open for 1% -> 0% of each run, Pallas kernels for 0% -> 0%
where the time goes in v1:
time: 87.2 us; the launch traced here: 87 us
  Pallas kernels  85.1 us (98%)
  local copies, waits for them, and re-layouts  1.87 us (2%)
    pallas_call x1, Pallas kernels, per_device(): pl.pallas_call(kernel, out_shape=jax.ShapeDtypeStruct((ROWS, COLS), BF16)...  85.1 us
    unnamed x1, local copies, waits for them, and re-layouts  1.87 us

profile of v1, /device:TPU:1, one launch (start us, length us, event | category | flops | bytes accessed | tf_op | source)
XLA Modules:
  0.0 87.0 jit_solution(1211017124890533909)
XLA Ops:
  0.0 85.1 %attention.1 = bf16[256,1024]{1,0:T(8,128)(2,1)} custom-call(bf16[256,512]{1,0:T(8,128)(2,1)} %q_hbm.1, bf16[256,512]{1,0:T(8,128)(2,1)} %k_hbm.1, bf16[256,512]{1,0:T(8,128)(2,1)} %v_hbm.1, bf16[512,8192]{1,0:T(8,128)(2,1)} %w_hbm.1), custom_call_target="tpu_custom_call" | custom-call | tf_op jit(solution)/shard_map/attention/pallas_call | solution.py:297
  85.1 1.9 %copy.6 = bf16[256,1024]{1,0:T(8,128)(2,1)} copy(bf16[256,1024]{1,0:T(8,128)(2,1)} %attention.1) | data formatting | bytes 1048576

commit v2 on v1

--- a/solution.py
+++ b/solution.py
@@ -27,9 +27,9 @@
 
 def kernel(
     q_hbm, k_hbm, v_hbm, w_hbm, out_ref,
-    src, qb, kv, wb, heads, obuf, acc, mx, sm, pbuf, ropp, rfin,
+    src, qkv, wb, heads, obuf, acc, mx, sm, pbuf, ropp, rfin,
     s_load, s_w, r_w, ss_w,
-    s_q, s_kv, r_q, r_kv,
+    s_z, r_z,
     s_x, r_x, s_rel, r_rel,
     s_o, r_o, s_oc, r_oc,
     s_p, r_p,
@@ -90,8 +90,7 @@
                 cd = (c + 1 - k) % NC
 
                 def go():
-                    remote(src.at[j, cd, 0], qb.at[z], s_q.at[j, k], r_q.at[z], dev(x, y, zd, cd)).start()
-                    remote(src.at[j, cd, pl.ds(1, 2)], kv.at[z, x * NC + cd], s_kv.at[j, k], r_kv.at[z], dev(x, y, zd, cd)).start()
+                    remote(src.at[j, cd], qkv.at[z, x * NC + cd], s_z.at[j, k], r_z.at[z], dev(x, y, zd, cd)).start()
 
                 if k == 0:
                     go()
@@ -100,8 +99,7 @@
 
                     @pl.when(zd == z)
                     def _():
-                        pltpu.make_async_copy(src.at[j, cd, 0], qb.at[z], r_q.at[z]).start()
-                        pltpu.make_async_copy(src.at[j, cd, pl.ds(1, 2)], kv.at[z, x * NC + cd], r_kv.at[z]).start()
+                        pltpu.make_async_copy(src.at[j, cd], qkv.at[z, x * NC + cd], r_z.at[z]).start()
 
         return carry
 
@@ -112,10 +110,16 @@
             w_hbm.at[:, pl.ds((n * NC + c) * COLS, COLS)], wb.at[n, c], s_w.at[n]
         ).start()
 
+    def pair(zs, xx, core):
+        return qkv.at[zs, xx * NC + core, pl.ds(1, 2)]
+
+    def one(zs, xx, n):
+        return qkv.at[zs, xx * NC + c, 1 + n]
+
     def unit(zq, zk, diagonal):
-        query = qb[zq]
-        key = kv[zk, :, 0].reshape(KEYS, HD)
-        value = kv[zk, :, 1].reshape(KEYS, HD)
+        query = qkv[zq, x * NC + c, 0]
+        key = qkv[zk, :, 1].reshape(KEYS, HD)
+        value = qkv[zk, :, 2].reshape(KEYS, HD)
         scores = lax.dot_general(query, key, (((1,), (1,)), ((), ())), preferred_element_type=F32)
         if diagonal:
             row = lax.broadcasted_iota(jnp.int32, scores.shape, 0)
@@ -133,9 +137,8 @@
         @pl.when(s < NZ)
         def _():
             zs = zof(s)
-            mine = kv.at[zs, x * NC + c]
-            wait_for(qb.at[zs], r_q.at[zs])
-            wait_for(mine, r_kv.at[zs])
+            mine = pair(zs, x, c)
+            wait_for(qkv.at[zs, x * NC + c], r_z.at[zs])
             remote(mine, mine, s_x.at[zs, 0], r_x.at[zs, 0], right).start()
             remote(mine, mine, s_x.at[zs, 1], r_x.at[zs, 1], left).start()
             remote(mine, mine, s_rel.at[zs, 0], r_rel.at[zs, 0], across).start()
@@ -143,26 +146,26 @@
         @pl.when((s >= 1) & (s < NZ + 1))
         def _():
             zs = zof(s - 1)
-            a = kv.at[zs, xl * NC + c]
+            a = pair(zs, xl, c)
             wait_for(a, r_x.at[zs, 0])
-            remote(a.at[0], a.at[0], s_x.at[zs, 2], r_x.at[zs, 2], right).start()
+            remote(one(zs, xl, 0), one(zs, xl, 0), s_x.at[zs, 2], r_x.at[zs, 2], right).start()
             remote(a, a, s_rel.at[zs, 1], r_rel.at[zs, 1], across).start()
-            b = kv.at[zs, xr * NC + c]
+            b = pair(zs, xr, c)
             wait_for(b, r_x.at[zs, 1])
-            remote(b.at[1], b.at[1], s_x.at[zs, 3], r_x.at[zs, 3], left).start()
+            remote(one(zs, xr, 1), one(zs, xr, 1), s_x.at[zs, 3], r_x.at[zs, 3], left).start()
             remote(b, b, s_rel.at[zs, 2], r_rel.at[zs, 2], across).start()
 
         @pl.when((s >= 2) & (s < NZ + 2))
         def _():
             zs = zof(s - 2)
-            o = kv.at[zs, xo * NC + c]
-            wait_for(o.at[0], r_x.at[zs, 2])
-            wait_for(o.at[1], r_x.at[zs, 3])
+            o = pair(zs, xo, c)
+            wait_for(one(zs, xo, 0), r_x.at[zs, 2])
+            wait_for(one(zs, xo, 1), r_x.at[zs, 3])
             remote(o, o, s_rel.at[zs, 3], r_rel.at[zs, 3], across).start()
 
-        @pl.when((s >= 2) & (s < 2 + NY))
-        def _():
-            n = s - 2
+        @pl.when(s >= NZ + 3 - NY)
+        def _():
+            n = s - (NZ + 3 - NY)
             remote(
                 w_hbm.at[:, pl.ds((n * NC + sib) * COLS, COLS)], wb.at[n, c], ss_w.at[n], r_w.at[n], across
             ).start()
@@ -172,7 +175,7 @@
             t = s - 3
             zs = zof(t)
             for n, xx in enumerate((x, xl, xr, xo)):
-                wait_for(kv.at[zs, xx * NC + sib], r_rel.at[zs, n])
+                wait_for(pair(zs, xx, sib), r_rel.at[zs, n])
             unit(zs, zs, True)
 
             def earlier(u, inner):
@@ -262,19 +265,16 @@
         @pl.when(zs // 4 == c)
         def _():
             j = zs - 4 * c
-            wait_for(src.at[j, sib, 0], s_q.at[j, 0])
-            wait_for(src.at[j, sib, pl.ds(1, 2)], s_kv.at[j, 0])
+            wait_for(src.at[j, sib], s_z.at[j, 0])
 
             @pl.when(zs != z)
             def _():
-                wait_for(src.at[j, c, 0], s_q.at[j, 1])
-                wait_for(src.at[j, c, pl.ds(1, 2)], s_kv.at[j, 1])
+                wait_for(src.at[j, c], s_z.at[j, 1])
 
         for n, xx in enumerate((x, x, xl, xr)):
-            part = kv.at[zs, xx * NC + c]
-            wait_for(part if n < 2 else part.at[n - 2], s_x.at[zs, n])
+            wait_for(pair(zs, xx, c) if n < 2 else one(zs, xx, n - 2), s_x.at[zs, n])
         for n, xx in enumerate((x, xl, xr, xo)):
-            wait_for(kv.at[zs, xx * NC + c], s_rel.at[zs, n])
+            wait_for(pair(zs, xx, c), s_rel.at[zs, n])
 
         @pl.when(zs != z)
         def _():
@@ -301,8 +301,7 @@
         out_specs=pl.BlockSpec(memory_space=pltpu.VMEM),
         scratch_shapes=[
             pltpu.VMEM((4, NC, 3, HALF, HD), BF16),
-            pltpu.VMEM((NZ, HALF, HD), BF16),
-            pltpu.VMEM((NZ, NX * NC, 2, HALF, HD), BF16),
+            pltpu.VMEM((NZ, NX * NC, 3, HALF, HD), BF16),
             pltpu.VMEM((NY, NC, 512, COLS), BF16),
             pltpu.VMEM((ROWS, NZ * HD), BF16),
             pltpu.VMEM((NZ, HALF, HD), BF16),
@@ -313,7 +312,7 @@
             pltpu.VMEM((NCH, ROWS, CHUNK), BF16),
             pltpu.VMEM((2, NCH, ROWS, CHUNK), BF16),
             dma((4, NC, 3)), dma((NY,)), dma((NY,)), dma((NY,)),
-            dma((4, NC)), dma((4, NC)), dma((NZ,)), dma((NZ,)),
+            dma((4, NC)), dma((NZ,)),
             dma((NZ, 4)), dma((NZ, 4)), dma((NZ, 4)), dma((NZ, 4)),
             dma((NZ,)), dma((NZ,)), dma((NZ,)), dma((NZ,)),
             dma((3, NCH)), dma((3, NCH)),

time: 87.2 us -> 87.1 us (level)
  no operation moved by 1% of the time
where the time goes in v2:
time: 87.1 us; the launch traced here: 86.9 us
  Pallas kernels  85 us (98%)
  local copies, waits for them, and re-layouts  1.87 us (2%)
    pallas_call x1, Pallas kernels, per_device(): pl.pallas_call(kernel, out_shape=jax.ShapeDtypeStruct((ROWS, COLS), BF16)...  85 us
    unnamed x1, local copies, waits for them, and re-layouts  1.87 us

profile of v2, /device:TPU:1, one launch (start us, length us, event | category | flops | bytes accessed | tf_op | source)
XLA Modules:
  0.0 86.9 jit_solution(12784621644322202219)
XLA Ops:
  0.0 85.0 %attention.1 = bf16[256,1024]{1,0:T(8,128)(2,1)} custom-call(bf16[256,512]{1,0:T(8,128)(2,1)} %q_hbm.1, bf16[256,512]{1,0:T(8,128)(2,1)} %k_hbm.1, bf16[256,512]{1,0:T(8,128)(2,1)} %v_hbm.1, bf16[512,8192]{1,0:T(8,128)(2,1)} %w_hbm.1), custom_call_target="tpu_custom_call" | custom-call | tf_op jit(solution)/shard_map/attention/pallas_call | solution.py:297
  85.1 1.9 %copy.6 = bf16[256,1024]{1,0:T(8,128)(2,1)} copy(bf16[256,1024]{1,0:T(8,128)(2,1)} %attention.1) | data formatting | bytes 1048576

commit v3 on v2

--- a/solution.py
+++ b/solution.py
@@ -133,6 +133,29 @@
         sm[zq] = sm[zq] * factor + jnp.sum(weights, axis=1, keepdims=True)
         acc[zq] = acc[zq] * factor + jnp.dot(weights.astype(BF16), value, preferred_element_type=F32)
 
+    last = (z + NZ // 2) % NZ
+
+    def send_rows(early):
+        def send_out(s, carry):
+            zs = zof(NZ - 1 - s)
+
+            @pl.when(zs < last if early else zs >= last)
+            def _():
+                obuf[zs] = (acc[zs] / sm[zs]).astype(BF16)
+                spot = heads.at[pl.ds(c * HALF, HALF), pl.ds(z * HD, HD)]
+
+                @pl.when(zs != z)
+                def _():
+                    remote(obuf.at[zs], spot, s_o.at[zs], r_o.at[z], dev(x, y, zs, c)).start()
+
+                @pl.when(zs == z)
+                def _():
+                    pltpu.make_async_copy(obuf.at[zs], spot, r_o.at[z]).start()
+
+            return carry
+
+        lax.fori_loop(0, NZ, send_out, 0)
+
     def step(s, carry):
         @pl.when(s < NZ)
         def _():
@@ -170,6 +193,10 @@
                 w_hbm.at[:, pl.ds((n * NC + sib) * COLS, COLS)], wb.at[n, c], ss_w.at[n], r_w.at[n], across
             ).start()
 
+        @pl.when(s == NZ + 2)
+        def _():
+            send_rows(True)
+
         @pl.when(s >= 3)
         def _():
             t = s - 3
@@ -189,22 +216,7 @@
 
     lax.fori_loop(0, NZ + 3, step, 0)
 
-    def send_out(s, carry):
-        zs = zof(NZ - 1 - s)
-        obuf[zs] = (acc[zs] / sm[zs]).astype(BF16)
-        spot = heads.at[pl.ds(c * HALF, HALF), pl.ds(z * HD, HD)]
-
-        @pl.when(zs != z)
-        def _():
-            remote(obuf.at[zs], spot, s_o.at[zs], r_o.at[z], dev(x, y, zs, c)).start()
-
-        @pl.when(zs == z)
-        def _():
-            pltpu.make_async_copy(obuf.at[zs], spot, r_o.at[z]).start()
-
-        return carry
-
-    lax.fori_loop(0, NZ, send_out, 0)
+    send_rows(False)
 
     def relay_out(s, carry):
         h = zof(s)

time: 87.1 us -> 84.8 us (0.974)
  Pallas kernels: 85 us -> 82.7 us
    pallas_call x1, Pallas kernels: 85 us -> 82.7 us  [per_device(): pl.pallas_call(kernel, out_shape=jax.ShapeDtypeStruct((ROWS, COLS), BF16)...]
where the time goes in v3:
time: 84.8 us; the launch traced here: 84.6 us
  Pallas kernels  82.7 us (98%)
  local copies, waits for them, and re-layouts  1.87 us (2%)
    pallas_call x1, Pallas kernels, per_device(): pl.pallas_call(kernel, out_shape=jax.ShapeDtypeStruct((ROWS, COLS), BF16)...  82.7 us
    unnamed x1, local copies, waits for them, and re-layouts  1.87 us

profile of v3, /device:TPU:1, one launch (start us, length us, event | category | flops | bytes accessed | tf_op | source)
XLA Modules:
  0.0 84.6 jit_solution(16484317349378232747)
XLA Ops:
  0.0 82.7 %attention.1 = bf16[256,1024]{1,0:T(8,128)(2,1)} custom-call(bf16[256,512]{1,0:T(8,128)(2,1)} %q_hbm.1, bf16[256,512]{1,0:T(8,128)(2,1)} %k_hbm.1, bf16[256,512]{1,0:T(8,128)(2,1)} %v_hbm.1, bf16[512,8192]{1,0:T(8,128)(2,1)} %w_hbm.1), custom_call_target="tpu_custom_call" | custom-call | tf_op jit(solution)/shard_map/attention/pallas_call | solution.py:309
  82.7 1.9 %copy.6 = bf16[256,1024]{1,0:T(8,128)(2,1)} copy(bf16[256,1024]{1,0:T(8,128)(2,1)} %attention.1) | data formatting | bytes 1048576
